TPU v7x, 32 devices: a whole 2x2x4 slice. The times are simulated.
32 devices in a mesh: slides: 2 (over y), rows: 4 (over z), cols: 2 (over x), chan: 2 (over core).
Axes of the slice: x: 2, y: 2, z: 4, core: 2. Of those that a mesh axis runs over, the one named last changes fastest.
Arguments:
- features: bfloat16 [128, 64, 384], P(('slides', 'rows'), 'cols', 'chan'), parts along dimension 0, may hold values from -6 to 6
- gate_input: bfloat16 [128, 64, 384], P(('slides', 'rows'), 'cols', 'chan'), parts along dimension 0, may hold values from -6 to 6
- decay_idx: int32 [128, 64], P(('slides', 'rows'), 'cols'), parts along dimension 0, may hold values from 0 to 15
- log_table: float32 [16, 384], P(None, 'chan'), may hold values from -1 to 0, as said below
- state_rate: float32 [16], replicated, may hold values from 0.5 to 2
- proj_row: bfloat16 [384, 32], P('chan'), may hold values from -0.0390625 to 0.0390625
- proj_col: bfloat16 [384, 32], P('chan'), may hold values from -0.0390625 to 0.0390625
- conv_w: float32 [3, 3, 384], P(None, None, 'chan'), may hold values from -0.5 to 0.5
- conv_b: float32 [384], P('chan'), may hold values from -0.5 to 0.5
- d_skip: float32 [384], P('chan'), may hold values from 0.5 to 1.5
Outputs:
- output: bfloat16 [128, 64, 384], P(('slides', 'rows'), 'cols', 'chan'), parts along dimension 0
There are 2 independent parts, one for each index of `slides`. A program takes and returns all parts, laid end to end along the dimension named above; an argument that names none is the same for every part. Nothing has to cross between parts.
Inputs may be any that keep to these rules, and one draw needn't show every extreme that they name: `log_table`: every entry is negative.
All inputs are finite; a program needn't handle non-finite values.
Results may differ from a plain program's by a relative error of at most 0.0061.
Values may be sent and summed in bfloat16 or wider, within the bound.
No kernel may reach another device: no remote copies, remote signals or barrier semaphores. Data moves between devices by JAX's collectives and lax.ppermute only.
A program may use at most 128 MiB of HBM per device.

v0:
```python
import jax
import jax.numpy as jnp
from jax import lax
from jax.sharding import PartitionSpec as P


def entering(shard, axis, combine, identity):
    size, position = (lax.axis_size(axis), lax.axis_index(axis))
    everything = jax.tree.map(lambda part: lax.all_gather(part, axis), shard)
    start = jax.tree.map(
        lambda part, zero: jnp.broadcast_to(jnp.asarray(zero, part.dtype), part.shape),
        shard,
        identity,
    )

    def step(k, before):
        reached = k < position
        new = combine(before, jax.tree.map(lambda part: part[k], everything))
        return jax.tree.map(lambda a, b: jnp.where(reached, a, b), new, before)

    return lax.fori_loop(0, size, step, start)


def extended(block, sides, width):
    for axis, dim in sides:
        count = lax.axis_size(axis)
        forward = [(i, i + 1) for i in range(count - 1)]
        backward = [(target, source) for source, target in forward]
        low = lax.ppermute(
            lax.slice_in_dim(block, block.shape[dim] - width, None, axis=dim), axis, forward
        )
        high = lax.ppermute(lax.slice_in_dim(block, 0, width, axis=dim), axis, backward)
        block = jnp.concatenate([low, block, high], axis=dim)
    return block


def combine_pair(earlier, latter):
    return (earlier[0] + latter[0], latter[1] + jnp.exp(latter[0]) * earlier[1])


def make_carry_combine(state_rate):
    rates = state_rate[:, None, None]

    def combine_carry(earlier, latter):
        return (earlier[0] + latter[0], latter[1] + jnp.exp(rates * latter[0][None]) * earlier[1])

    return combine_carry


def lookup(decay_idx, log_table):
    entries = log_table.shape[0]
    onehot = (decay_idx[..., None] == jnp.arange(entries, dtype=jnp.int32)).astype(jnp.float32)
    return jnp.einsum("hwk,ke->hwe", onehot, log_table, precision=lax.Precision.HIGHEST)


def tile_states(values, log_decays, coeffs, state_rate, scan_axis):
    num_states = state_rate.shape[0]
    drive_cols = jnp.moveaxis(coeffs[..., :num_states], -1, 0)[..., None]
    log_sums = jnp.cumsum(log_decays, axis=scan_axis)

    def one_state(inputs):
        state_scale, drive_col = inputs
        unused, states = lax.associative_scan(
            combine_pair, (log_decays * state_scale, drive_col * values), axis=scan_axis
        )
        return states

    return (log_sums, lax.map(one_state, (state_rate, drive_cols)))


def finish(log_sums, states, inflow, coeffs, state_rate):
    num_states = states.shape[0]
    outputs = jnp.moveaxis(coeffs[..., num_states:], -1, 0)[..., None]
    carried = jnp.exp(state_rate[:, None, None, None] * log_sums[None]) * inflow
    return jnp.sum(outputs * (states + carried), axis=0)


def column_coeffs(middle, proj_col):
    return lax.psum(jnp.dot(middle, proj_col, preferred_element_type=jnp.float32), "chan")


def shards(
    features,
    gate_input,
    decay_idx,
    log_table,
    state_rate,
    proj_row,
    proj_col,
    conv_w,
    conv_b,
    d_skip,
):
    combine_carry = make_carry_combine(state_rate)
    log_decays = lookup(decay_idx, log_table)
    feats_wide = features.astype(jnp.float32)
    coeff_row = lax.psum(jnp.dot(features, proj_row, preferred_element_type=jnp.float32), "chan")
    row_sums, states = tile_states(feats_wide, log_decays, coeff_row, state_rate, 1)
    tile_ends = (row_sums[:, -1, :], states[:, :, -1, :])
    incoming = entering(
        tile_ends,
        "cols",
        combine_carry,
        (jnp.zeros_like(tile_ends[0]), jnp.zeros_like(tile_ends[1])),
    )
    swept_rows = finish(row_sums, states, incoming[1][:, :, None, :], coeff_row, state_rate)
    row_out = (swept_rows + d_skip * feats_wide).astype(jnp.bfloat16)
    padded = extended(row_out, (("rows", 0), ("cols", 1)), 1).astype(jnp.float32)
    tile_rows = row_out.shape[0]
    tile_cols = row_out.shape[1]
    convolved = jnp.zeros(row_out.shape, jnp.float32) + conv_b
    for offset_row in range(3):
        for offset_col in range(3):
            convolved = (
                convolved
                + conv_w[offset_row, offset_col]
                * padded[offset_row : offset_row + tile_rows, offset_col : offset_col + tile_cols]
            )
    middle = jax.nn.silu(convolved).astype(jnp.bfloat16)
    strip_vals = lax.all_to_all(middle, "rows", split_axis=1, concat_axis=0, tiled=True)
    strip_index = lax.all_to_all(decay_idx, "rows", split_axis=1, concat_axis=0, tiled=True)
    strip_decays = lookup(strip_index, log_table)
    strip_wide = strip_vals.astype(jnp.float32)
    coeff_col = column_coeffs(strip_vals, proj_col)
    col_sums, states = tile_states(strip_wide, strip_decays, coeff_col, state_rate, 0)
    strip_out = (
        finish(col_sums, states, jnp.zeros((), jnp.float32), coeff_col, state_rate)
        + d_skip * strip_wide
    )
    combined = lax.all_to_all(strip_out, "rows", split_axis=0, concat_axis=1, tiled=True)
    return (combined * jax.nn.silu(gate_input.astype(jnp.float32))).astype(jnp.bfloat16)


def solution(mesh):
    placed = (
        P(("slides", "rows"), "cols", "chan"),
        P(("slides", "rows"), "cols", "chan"),
        P(("slides", "rows"), "cols"),
        P(None, "chan"),
        P(),
        P("chan", None),
        P("chan", None),
        P(None, None, "chan"),
        P("chan"),
        P("chan"),
    )
    return jax.shard_map(
        shards,
        mesh=mesh,
        in_specs=placed,
        out_specs=P(("slides", "rows"), "cols", "chan"),
        check_vma=False,
    )
```

profile of v0, /device:TPU:0, one launch (start us, length us, event | category | flops | bytes accessed | tf_op | source)
XLA Modules:
  0.0 399.4 jit_solution(8053558625621068115)
XLA Ops:
  6.5 1.9 fusion.42
  9.9 6.3 %all-to-all-start.1 = ((s32[4,1,128]{2,1,0:T(1,128)}), s32[4,1,128]{2,1,0:T(1,128)S(1)}, u32[]{:S(2)}, u32[]{:S(2)}) async-start(s32[4,1,128]{2,1,0:T(1,128)} %reshape.23), calls=%async_computation.1 | async-start | bytes 4096 | tf_op jit(solution)/shard_map/all_to_all | solution.py:121
  20.7 4.4 %all-gather.1 = f32[32,1,192]{2,0,1:T(8,128)S(1)} all-gather(f32[16,1,192]{2,0,1:T(8,128)S(1)} %slice.400), channel_id=3, replica_groups=mesh['slides'=2,'rows'=4,'cols'=2,'chan'=2] {'cols'}, dimensions={0}, use_global_device_ids=true | all-gather | bytes 36864 | tf_op jit(solution)/shard_map/all_gather | solution.py:9
  25.1 5.5 %all-reduce.25.cloned.1.call-done = f32[16,32,32]{2,1,0:T(8,128)} async-done(((f32[16,32,32]{2,1,0:T(8,128)}), f32[16,32,32]{2,1,0:T(8,128)}) %all-reduce.25.cloned.1.call-update) | async-done | bytes 65552 | tf_op jit(solution)/shard_map/psum | solution.py:97
  30.6 1.9 slice_bitcast_fusion.3
  33.3 179.7 %while.37 = (s32[]{:T(128)}, f32[16,16,32,192]{3,2,1,0:T(8,128)}, f32[16,16,32,1]{2,1,3,0:T(8,128)}, f32[16,32,192]{2,1,0:T(8,128)}, f32[16]{0:T(128)}, /*index=5*/f32[16,32,192]{2,1,0:T(8,128)S(1)}) while((s32[]{:T(128)}, f32[16,16,32,192]{3,2,1,0:T(8,128)}, f32[16,16,32,1]{2,1,3,0:T(8,128)}, f32[16,32,192]{2,1,0:T(8,128)}, ...), condition=%wide.region_2.3_spmd.clone, body=%wide.region_1.0_spmd.sunk.clone | while | flops 998402 | bytes 15030905 | solution.py:68
  35.3 1.9 broadcast_multiply_fusion.8
  46.5 1.9 broadcast_multiply_fusion.8
  136.3 1.9 broadcast_multiply_fusion.8
  192.4 1.9 broadcast_multiply_fusion.8
  212.9 9.9 %copy.50 = f32[16,16,32,192]{3,1,2,0:T(8,128)S(1)} copy(f32[16,16,32,192]{3,2,1,0:T(8,128)} %get-tuple-element.178) | data formatting | bytes 12582912 | tf_op jit(solution)/shard_map/while | solution.py:68
  223.0 9.5 %all-gather = f32[32,16,1,192]{3,1,2,0:T(8,128)S(1)} all-gather(f32[16,16,1,192]{3,1,2,0:T(8,128)S(1)} %slice.399), channel_id=2, replica_groups=mesh['slides'=2,'rows'=4,'cols'=2,'chan'=2] {'cols'}, dimensions={0}, use_global_device_ids=true | all-gather | bytes 589824 | tf_op jit(solution)/shard_map/all_gather | solution.py:9
  232.9 4.8 %multiply_reduce_fusion.1 = f32[16,32,192]{2,1,0:T(8,128)S(1)} fusion(f32[16,16,32,192]{3,2,1,0:T(8,128)} %get-tuple-element.178, f32[16,16,192]{2,1,0:T(8,128)S(1)} %get-tuple-element.179, f32[16,32,192]{2,1,0:T(8,128)S(1)} %copy-done.4, f32[16]{0:T(128)S(1)} %bitcast.166, f32[16,16,32]{2,1,0:T(8,128)S(1)} %copy.46), kind=kLoop, calls=%fused_computation.70 | loop fusion | flops 7766016 | bytes 7307328 | tf_op jit(solution)/shard_map/reduce_sum | solution.py:75
  237.9 3.7 collective-permute-start
  244.2 3.0 collective-permute-done.1
  247.2 3.4 collective-permute-start.2
  252.0 4.2 %collective-permute-done.3 = bf16[18,1,192]{2,1,0:T(2,128)(2,1)S(1)} collective-permute-done((bf16[18,1,192]{2,1,0:T(2,128)(2,1)S(1)}, bf16[18,1,192]{2,1,0:T(2,128)(2,1)S(1)}, u32[]{:S(2)}, u32[]{:S(2)}) %collective-permute-start.3) | collective-permute-done | bytes 6944 | tf_op jit(solution)/shard_map/ppermute | solution.py:32
  257.8 3.7 all-to-all-start
  262.8 5.4 %all-to-all-done = bf16[16,32,192]{2,0,1:T(8,128)(2,1)S(1)} async-done(((bf16[16,32,192]{2,0,1:T(8,128)(2,1)}), bf16[16,32,192]{2,0,1:T(8,128)(2,1)S(1)}, u32[]{:S(2)}, u32[]{:S(2)}) %all-to-all-start) | async-done | bytes 196640 | tf_op jit(solution)/shard_map/all_to_all | solution.py:120
  269.3 17.2 %all-reduce.27.cloned.1.call-done = f32[64,8,32]{2,1,0:T(8,128)} async-done(((f32[64,8,32]{2,1,0:T(8,128)}), f32[64,8,32]{2,1,0:T(8,128)}) %all-reduce.27.cloned.1.call-update) | async-done | bytes 65552 | tf_op jit(solution)/shard_map/psum | solution.py:79
  286.5 1.9 slice_bitcast_fusion.1
  289.6 76.2 %while.38 = (s32[]{:T(128)}, f32[16,64,8,192]{3,2,1,0:T(8,128)}, f32[16,64,8,1]{2,1,3,0:T(8,128)}, f32[64,8,192]{2,1,0:T(8,128)S(1)}, f32[16]{0:T(128)S(1)}, /*index=5*/f32[64,8,192]{2,1,0:T(8,128)S(1)}) while((s32[]{:T(128)}, f32[16,64,8,192]{3,2,1,0:T(8,128)}, f32[16,64,8,1]{2,1,3,0:T(8,128)}, f32[64,8,192]{2,1,0:T(8,128)S(1)}, ...), condition=%wide.region_9.10_spmd.clone, body=%wide.region_8.9_spmd.sunk.clone | while | flops 1035266 | bytes 11215489 | solution.py:68
  367.3 4.7 %multiply_reduce_fusion = f32[64,8,192]{2,1,0:T(8,128)S(1)} fusion(f32[16,64,8,192]{3,2,1,0:T(8,128)} %get-tuple-element.180, f32[64,8,192]{2,1,0:T(8,128)} %fusion.52, f32[16]{0:T(128)S(1)} %get-tuple-element.646, f32[16,64,8]{2,1,0:T(8,128)S(1)} %copy.53), kind=kLoop, calls=%fused_computation.69 | loop fusion | flops 7766016 | bytes 7110720 | tf_op jit(solution)/shard_map/reduce_sum | solution.py:75
  372.1 19.6 %all_to_all.52 = f32[64,8,192]{2,1,0:T(8,128)S(1)} all-to-all(f32[64,8,192]{2,1,0:T(8,128)S(1)} %multiply_add_fusion.9), channel_id=1, replica_groups=mesh['slides'=2,'rows'=4,'cols'=2,'chan'=2] {'rows'}, dimensions={0} | all-to-all | bytes 786432 | tf_op jit(solution)/shard_map/all_to_all | solution.py:130
  (1557 shorter events, 257.6 us)
Async XLA Ops:
  6.5 9.7 %copy-start = (f32[16,192]{1,0:T(8,128)S(1)}, f32[16,192]{1,0:T(8,128)}, u32[]{:S(2)}) copy-start(f32[16,192]{1,0:T(8,128)} %param.19) | copy-start | bytes 36868
  6.5 24.1 %all-reduce.25.cloned.1.call-start = ((), (), s32[]{:S(2)}) async-start(), calls=%async_computation.3 | async-start | bytes 524288 | tf_op jit(solution)/shard_map/psum | solution.py:97
  9.9 233.0 %all-to-all-start.1 = ((s32[4,1,128]{2,1,0:T(1,128)}), s32[4,1,128]{2,1,0:T(1,128)S(1)}, u32[]{:S(2)}, u32[]{:S(2)}) async-start(s32[4,1,128]{2,1,0:T(1,128)} %reshape.23), calls=%async_computation.1 | async-start | bytes 4096 | tf_op jit(solution)/shard_map/all_to_all | solution.py:121
  212.9 19.5 %copy-start.7 = (f32[16]{0:T(128)S(1)}, f32[16]{0:T(128)}, u32[]{:S(2)}) copy-start(f32[16]{0:T(128)} %get-tuple-element.644) | copy-start | bytes 196
  212.9 19.8 %copy-start.5 = (f32[16,16,32]{0,2,1:T(8,128)S(1)}, f32[16,16,32]{0,2,1:T(8,128)}, u32[]{:S(2)}) copy-start(f32[16,16,32]{0,2,1:T(8,128)} %get-tuple-element.321) | copy-start | bytes 98308
  212.9 20.0 %copy-start.4 = (f32[16,32,192]{2,1,0:T(8,128)S(1)}, f32[16,32,192]{2,1,0:T(8,128)}, u32[]{:S(2)}) copy-start(f32[16,32,192]{2,1,0:T(8,128)} %copy.49) | copy-start | bytes 1179652
  222.9 14.9 %copy-start.3 = (bf16[16,32,192]{2,1,0:T(8,128)(2,1)S(1)}, bf16[16,32,192]{2,1,0:T(8,128)(2,1)}, u32[]{:S(2)}) copy-start(bf16[16,32,192]{2,1,0:T(8,128)(2,1)} %param.16) | copy-start | bytes 589828
  222.9 14.9 %copy-start.10 = (f32[192]{0:T(256)S(1)}, f32[192]{0:T(256)}, u32[]{:S(2)}) copy-start(f32[192]{0:T(256)} %param.25) | copy-start | bytes 2308
  222.9 19.9 %copy-start.9 = (f32[3,3,192]{2,1,0:T(4,128)S(1)}, f32[3,3,192]{2,1,0:T(4,128)}, u32[]{:S(2)}) copy-start(f32[3,3,192]{2,1,0:T(4,128)} %param.23) | copy-start | bytes 20740
  232.4 24.0 %copy-start.11 = (f32[192]{0:T(256)S(1)}, f32[192]{0:T(256)}, u32[]{:S(2)}) copy-start(f32[192]{0:T(256)} %param.24) | copy-start | bytes 2308
  232.9 35.4 %copy-start.8 = (bf16[192,32]{0,1:T(8,128)(2,1)S(1)}, bf16[192,32]{0,1:T(8,128)(2,1)}, u32[]{:S(2)}) copy-start(bf16[192,32]{0,1:T(8,128)(2,1)} %param.22) | copy-start | bytes 36868
  237.9 6.3 %collective-permute-start = (bf16[1,32,192]{2,1,0:T(8,128)(2,1)S(1)}, bf16[1,32,192]{2,1,0:T(8,128)(2,1)S(1)}, u32[]{:S(2)}, u32[]{:S(2)}) collective-permute-start(bf16[1,32,192]{2,1,0:T(8,128)(2,1)S(1)} %get-tuple-element.319), channel_id=1, source_target_pairs={{0,4},{4,8},{8,12},{1,5},{5,9},{9,13},{2,6},{6,10},{10,14},{3,7},{... | collective-permute-start | bytes 36872 | tf_op jit(solution)/shard_map/ppermute | solution.py:29
  241.5 5.6 %collective-permute-start.1 = (bf16[1,32,192]{2,1,0:T(8,128)(2,1)S(1)}, bf16[1,32,192]{2,1,0:T(8,128)(2,1)S(1)}, u32[]{:S(2)}, u32[]{:S(2)}) collective-permute-start(bf16[1,32,192]{2,1,0:T(8,128)(2,1)S(1)} %get-tuple-element.320), channel_id=1, source_target_pairs={{4,0},{8,4},{12,8},{5,1},{9,5},{13,9},{6,2},{10,6},{14,10},{7,3},{... | collective-permute-start | bytes 36872 | tf_op jit(solution)/shard_map/ppermute | solution.py:32
  247.2 4.8 %collective-permute-start.2 = (bf16[18,1,192]{2,1,0:T(2,128)(2,1)S(1)}, bf16[18,1,192]{2,1,0:T(2,128)(2,1)S(1)}, u32[]{:S(2)}, u32[]{:S(2)}) collective-permute-start(bf16[18,1,192]{2,1,0:T(2,128)(2,1)S(1)} %get-tuple-element.315), channel_id=1, source_target_pairs={{0,2},{1,3},{4,6},{5,7},{8,10},{9,11},{12,14},{13,15},{16,18},{17,... | collective-permute-start | bytes 20744 | tf_op jit(solution)/shard_map/ppermute | solution.py:29
  250.6 5.7 %collective-permute-start.3 = (bf16[18,1,192]{2,1,0:T(2,128)(2,1)S(1)}, bf16[18,1,192]{2,1,0:T(2,128)(2,1)S(1)}, u32[]{:S(2)}, u32[]{:S(2)}) collective-permute-start(bf16[18,1,192]{2,1,0:T(2,128)(2,1)S(1)} %get-tuple-element.316), channel_id=1, source_target_pairs={{2,0},{3,1},{6,4},{7,5},{10,8},{11,9},{14,12},{15,13},{18,16},{19,... | collective-permute-start | bytes 20744 | tf_op jit(solution)/shard_map/ppermute | solution.py:32
  257.8 10.5 %all-to-all-start = ((bf16[16,32,192]{2,0,1:T(8,128)(2,1)}), bf16[16,32,192]{2,0,1:T(8,128)(2,1)S(1)}, u32[]{:S(2)}, u32[]{:S(2)}) async-start(bf16[16,32,192]{2,0,1:T(8,128)(2,1)} %copy.51), calls=%async_computation | async-start | bytes 524288 | tf_op jit(solution)/shard_map/all_to_all | solution.py:120
  261.4 25.0 %all-reduce.27.cloned.1.call-start = ((), (), s32[]{:S(2)}) async-start(), calls=%async_computation.4 | async-start | bytes 524288 | tf_op jit(solution)/shard_map/psum | solution.py:79
  268.3 21.3 %copy-start.1 = (bf16[16,4,8,192]{3,2,0,1:T(8,128)(2,1)}, bf16[16,4,8,192]{3,2,0,1:T(8,128)(2,1)S(1)}, u32[]{:S(2)}) copy-start(bf16[16,4,8,192]{3,2,0,1:T(8,128)(2,1)S(1)} %copy.52) | copy-start | bytes 589828
  365.8 6.2 %copy-start.2 = (bf16[16,4,8,192]{3,2,0,1:T(8,128)(2,1)S(1)}, bf16[16,4,8,192]{3,2,0,1:T(8,128)(2,1)}, u32[]{:S(2)}) copy-start(bf16[16,4,8,192]{3,2,0,1:T(8,128)(2,1)} %copy-done.1) | copy-start | bytes 589828
  365.8 25.9 %copy-start.6 = (bf16[16,32,192]{2,1,0:T(8,128)(2,1)S(1)}, bf16[16,32,192]{2,1,0:T(8,128)(2,1)}, u32[]{:S(2)}) copy-start(bf16[16,32,192]{2,1,0:T(8,128)(2,1)} %param.17) | copy-start | bytes 589828
Sparse Core Ops, SparseCore 0:
  9.7 20.9 all-reduce.24
  269.4 17.0 all-reduce.26
where the time goes:
time: 403 us; the launch traced here: 399 us
  local copies, waits for them, and re-layouts  178 us (44%)
  other arithmetic  104 us (26%)
  waiting for transfers between devices  35.4 us (9%)
  blocking collectives  33.5 us (8%)
  starting transfers between devices  19.6 us (5%)
  between operations  13.7 us (3%)
  loops' own time  10.1 us (3%)
  matrix products  4.34 us (1%)
    slice x464, local copies, waits for them, and re-layouts, one_state(): lax.associative_scan(combine_pair, (log_decays * state_scale, drive_col *...  66 us
    mul x32, other arithmetic, one_state(): log_decays * state_scale  41.8 us
    pad x288, local copies, waits for them, and re-layouts, one_state(): lax.associative_scan(combine_pair, (log_decays * state_scale, drive_col *...  36.8 us
    dynamic_slice x32, local copies, waits for them, and re-layouts, tile_states(): return (log_sums, lax.map(one_state, (state_rate, drive_cols)))  30.6 us
    dynamic_update_slice x32, other arithmetic, tile_states(): return (log_sums, lax.map(one_state, (state_rate, drive_cols)))  28.1 us
    mul x32, local copies, waits for them, and re-layouts, one_state(): drive_col * values  23.3 us
    all_to_all x1, blocking collectives, shards(): lax.all_to_all(strip_out, 'rows', split_axis=0, concat_axis=1, tiled=True)  19.6 us
    psum x1, waiting for transfers between devices, column_coeffs(): lax.psum(jnp.dot(middle, proj_col, preferred_element_type=jnp.float32), '...  17.2 us
  transfers between devices with their start and end apart: 8, of which 6 were waited for; matrix products, arithmetic and copies ran while one was open for 50% of the time, Pallas kernels for 0%

commit v1 on v0

--- a/solution.py
+++ b/solution.py
@@ -2,6 +2,7 @@
 import jax.numpy as jnp
 from jax import lax
 from jax.sharding import PartitionSpec as P
+from jax.lax import all_gather
 
 
 def entering(shard, axis, combine, identity):
@@ -76,7 +77,10 @@
 
 
 def column_coeffs(middle, proj_col):
-    return lax.psum(jnp.dot(middle, proj_col, preferred_element_type=jnp.float32), "chan")
+    return jnp.sum(
+        all_gather(jnp.dot(middle, proj_col, preferred_element_type=jnp.float32), axis_name="chan"),
+        axis=0,
+    )
 
 
 def shards(

time: 403 us -> 383 us (0.950)
  waiting for transfers between devices: 35.4 us -> 18.2 us
    psum x1 -> x0, waiting for transfers between devices: 17.2 us -> none  [column_coeffs(): lax.psum(jnp.dot(middle, proj_col, preferred_element_type=jnp.float32), '...]
  transfers between devices with their start and end apart: 8 -> 7, of which waited for: 6 -> 5; matrix products, arithmetic and copies ran while one was open for 50% -> 52% of each run, Pallas kernels for 0% -> 0%
where the time goes in v1:
time: 383 us; the launch traced here: 379 us
  local copies, waits for them, and re-layouts  177 us (46%)
  other arithmetic  103 us (27%)
  blocking collectives  34.1 us (9%)
  starting transfers between devices  19.6 us (5%)
  waiting for transfers between devices  18.2 us (5%)
  between operations  13.7 us (4%)
  loops' own time  10.1 us (3%)
    slice x464, local copies, waits for them, and re-layouts, one_state(): lax.associative_scan(combine_pair, (log_decays * state_scale, drive_col *...  66 us
    mul x32, other arithmetic, one_state(): log_decays * state_scale  40.4 us
    pad x288, local copies, waits for them, and re-layouts, one_state(): lax.associative_scan(combine_pair, (log_decays * state_scale, drive_col *...  36.8 us
    dynamic_slice x32, local copies, waits for them, and re-layouts, tile_states(): return (log_sums, lax.map(one_state, (state_rate, drive_cols)))  29.3 us
    dynamic_update_slice x32, other arithmetic, tile_states(): return (log_sums, lax.map(one_state, (state_rate, drive_cols)))  28.1 us
    mul x32, local copies, waits for them, and re-layouts, one_state(): drive_col * values  23.3 us
    all_to_all x1, blocking collectives, shards(): lax.all_to_all(strip_out, 'rows', split_axis=0, concat_axis=1, tiled=True)  18 us
    all_gather x2, blocking collectives, entering(): everything = jax.tree.map(lambda part: lax.all_gather(part, axis), shard)  13.9 us
  transfers between devices with their start and end apart: 7, of which 5 were waited for; matrix products, arithmetic and copies ran while one was open for 52% of the time, Pallas kernels for 0%

profile of v1, /device:TPU:0, one launch (start us, length us, event | category | flops | bytes accessed | tf_op | source)
XLA Modules:
  0.0 379.1 jit_solution(2541651660457045248)
XLA Ops:
  6.5 1.9 fusion.42
  9.9 6.3 %all-to-all-start.1 = ((s32[4,1,128]{2,1,0:T(1,128)}), s32[4,1,128]{2,1,0:T(1,128)S(1)}, u32[]{:S(2)}, u32[]{:S(2)}) async-start(s32[4,1,128]{2,1,0:T(1,128)} %reshape.24), calls=%async_computation.1 | async-start | bytes 4096 | tf_op jit(solution)/shard_map/all_to_all | solution.py:125
  17.8 1.8 convert_element_type.23
  20.7 4.4 %all-gather.1 = f32[32,1,192]{2,0,1:T(8,128)S(1)} all-gather(f32[16,1,192]{2,0,1:T(8,128)S(1)} %slice.400), channel_id=3, replica_groups=mesh['slides'=2,'rows'=4,'cols'=2,'chan'=2] {'cols'}, dimensions={0}, use_global_device_ids=true | all-gather | bytes 36864 | tf_op jit(solution)/shard_map/all_gather | solution.py:10
  25.1 5.5 %all-reduce.24.cloned.1.call-done = f32[16,32,32]{2,1,0:T(8,128)} async-done(((f32[16,32,32]{2,1,0:T(8,128)}), f32[16,32,32]{2,1,0:T(8,128)}) %all-reduce.24.cloned.1.call-update) | async-done | bytes 65552 | tf_op jit(solution)/shard_map/psum | solution.py:101
  30.6 1.9 slice_bitcast_fusion.3
  33.3 177.3 %while.37 = (s32[]{:T(128)}, f32[16,16,32,192]{3,2,1,0:T(8,128)}, f32[16,16,32,1]{2,1,3,0:T(8,128)}, f32[16,32,192]{2,1,0:T(8,128)}, f32[16]{0:T(128)}, /*index=5*/f32[16,32,192]{2,1,0:T(8,128)S(1)}) while((s32[]{:T(128)}, f32[16,16,32,192]{3,2,1,0:T(8,128)}, f32[16,16,32,1]{2,1,3,0:T(8,128)}, f32[16,32,192]{2,1,0:T(8,128)}, ...), condition=%wide.region_2.3_spmd.clone, body=%wide.region_1.0_spmd.sunk.clone | while | flops 998402 | bytes 15030905 | solution.py:69
  35.2 1.8 broadcast_multiply_fusion.8
  46.3 1.8 broadcast_multiply_fusion.8
  79.6 1.8 broadcast_multiply_fusion.8
  90.6 1.8 broadcast_multiply_fusion.8
  210.6 9.9 %copy.46 = f32[16,16,32,192]{3,1,2,0:T(8,128)S(1)} copy(f32[16,16,32,192]{3,2,1,0:T(8,128)} %get-tuple-element.178) | data formatting | bytes 12582912 | tf_op jit(solution)/shard_map/while | solution.py:69
  220.6 9.5 %all-gather = f32[32,16,1,192]{3,1,2,0:T(8,128)S(1)} all-gather(f32[16,16,1,192]{3,1,2,0:T(8,128)S(1)} %slice.399), channel_id=2, replica_groups=mesh['slides'=2,'rows'=4,'cols'=2,'chan'=2] {'cols'}, dimensions={0}, use_global_device_ids=true | all-gather | bytes 589824 | tf_op jit(solution)/shard_map/all_gather | solution.py:10
  230.6 4.8 %multiply_reduce_fusion.1 = f32[16,32,192]{2,1,0:T(8,128)S(1)} fusion(f32[16,16,32,192]{3,2,1,0:T(8,128)} %get-tuple-element.178, f32[16,16,192]{2,1,0:T(8,128)S(1)} %get-tuple-element.179, f32[16,32,192]{2,1,0:T(8,128)S(1)} %copy-done.4, f32[16]{0:T(128)S(1)} %bitcast.168, f32[16,16,32]{2,1,0:T(8,128)S(1)} %copy.42), kind=kLoop, calls=%fused_computation.70 | loop fusion | flops 7766016 | bytes 7307328 | tf_op jit(solution)/shard_map/reduce_sum | solution.py:76
  235.5 3.7 collective-permute-start
  241.8 3.0 collective-permute-done.1
  244.8 3.4 collective-permute-start.2
  249.7 4.2 %collective-permute-done.3 = bf16[18,1,192]{2,1,0:T(2,128)(2,1)S(1)} collective-permute-done((bf16[18,1,192]{2,1,0:T(2,128)(2,1)S(1)}, bf16[18,1,192]{2,1,0:T(2,128)(2,1)S(1)}, u32[]{:S(2)}, u32[]{:S(2)}) %collective-permute-start.3) | collective-permute-done | bytes 6944 | tf_op jit(solution)/shard_map/ppermute | solution.py:33
  255.4 3.7 all-to-all-start
  260.4 5.4 %all-to-all-done = bf16[16,32,192]{2,0,1:T(8,128)(2,1)S(1)} async-done(((bf16[16,32,192]{2,0,1:T(8,128)(2,1)}), bf16[16,32,192]{2,0,1:T(8,128)(2,1)S(1)}, u32[]{:S(2)}, u32[]{:S(2)}) %all-to-all-start) | async-done | bytes 196640 | tf_op jit(solution)/shard_map/all_to_all | solution.py:124
  266.8 2.2 all-gather.2
  271.1 75.9 %while.38 = (s32[]{:T(128)}, f32[16,64,8,192]{3,2,1,0:T(8,128)}, f32[16,64,8,1]{2,1,3,0:T(8,128)}, f32[64,8,192]{2,1,0:T(8,128)S(1)}, f32[16]{0:T(128)S(1)}, /*index=5*/f32[64,8,192]{2,1,0:T(8,128)S(1)}) while((s32[]{:T(128)}, f32[16,64,8,192]{3,2,1,0:T(8,128)}, f32[16,64,8,1]{2,1,3,0:T(8,128)}, f32[64,8,192]{2,1,0:T(8,128)S(1)}, ...), condition=%wide.region_9.10_spmd.clone, body=%wide.region_8.9_spmd.sunk.clone | while | flops 1035266 | bytes 11215489 | solution.py:69
  348.6 4.7 %multiply_reduce_fusion = f32[64,8,192]{2,1,0:T(8,128)S(1)} fusion(f32[16,64,8,192]{3,2,1,0:T(8,128)} %get-tuple-element.180, f32[64,8,192]{2,1,0:T(8,128)} %fusion.52, f32[16]{0:T(128)S(1)} %get-tuple-element.630, f32[16,64,8]{2,1,0:T(8,128)S(1)} %copy.49), kind=kLoop, calls=%fused_computation.69 | loop fusion | flops 7766016 | bytes 7110720 | tf_op jit(solution)/shard_map/reduce_sum | solution.py:76
  353.4 18.0 %all_to_all.52 = f32[64,8,192]{2,1,0:T(8,128)S(1)} all-to-all(f32[64,8,192]{2,1,0:T(8,128)S(1)} %multiply_add_fusion.9), channel_id=1, replica_groups=mesh['slides'=2,'rows'=4,'cols'=2,'chan'=2] {'rows'}, dimensions={0} | all-to-all | bytes 786432 | tf_op jit(solution)/shard_map/all_to_all | solution.py:134
  (1556 shorter events, 254.3 us)
Async XLA Ops:
  6.5 9.7 %copy-start = (f32[16,192]{1,0:T(8,128)S(1)}, f32[16,192]{1,0:T(8,128)}, u32[]{:S(2)}) copy-start(f32[16,192]{1,0:T(8,128)} %param.19) | copy-start | bytes 36868
  6.5 24.1 %all-reduce.24.cloned.1.call-start = ((), (), s32[]{:S(2)}) async-start(), calls=%async_computation.3 | async-start | bytes 524288 | tf_op jit(solution)/shard_map/psum | solution.py:101
  9.9 230.6 %all-to-all-start.1 = ((s32[4,1,128]{2,1,0:T(1,128)}), s32[4,1,128]{2,1,0:T(1,128)S(1)}, u32[]{:S(2)}, u32[]{:S(2)}) async-start(s32[4,1,128]{2,1,0:T(1,128)} %reshape.24), calls=%async_computation.1 | async-start | bytes 4096 | tf_op jit(solution)/shard_map/all_to_all | solution.py:125
  210.6 19.5 %copy-start.7 = (f32[16]{0:T(128)S(1)}, f32[16]{0:T(128)}, u32[]{:S(2)}) copy-start(f32[16]{0:T(128)} %get-tuple-element.628) | copy-start | bytes 196
  210.6 19.8 %copy-start.5 = (f32[16,16,32]{0,2,1:T(8,128)S(1)}, f32[16,16,32]{0,2,1:T(8,128)}, u32[]{:S(2)}) copy-start(f32[16,16,32]{0,2,1:T(8,128)} %get-tuple-element.309) | copy-start | bytes 98308
  210.6 20.0 %copy-start.4 = (f32[16,32,192]{2,1,0:T(8,128)S(1)}, f32[16,32,192]{2,1,0:T(8,128)}, u32[]{:S(2)}) copy-start(f32[16,32,192]{2,1,0:T(8,128)} %copy.45) | copy-start | bytes 1179652
  220.5 14.9 %copy-start.3 = (bf16[16,32,192]{2,1,0:T(8,128)(2,1)S(1)}, bf16[16,32,192]{2,1,0:T(8,128)(2,1)}, u32[]{:S(2)}) copy-start(bf16[16,32,192]{2,1,0:T(8,128)(2,1)} %param.16) | copy-start | bytes 589828
  220.5 14.9 %copy-start.10 = (f32[192]{0:T(256)S(1)}, f32[192]{0:T(256)}, u32[]{:S(2)}) copy-start(f32[192]{0:T(256)} %param.25) | copy-start | bytes 2308
  220.5 19.9 %copy-start.9 = (f32[3,3,192]{2,1,0:T(4,128)S(1)}, f32[3,3,192]{2,1,0:T(4,128)}, u32[]{:S(2)}) copy-start(f32[3,3,192]{2,1,0:T(4,128)} %param.23) | copy-start | bytes 20740
  230.0 24.0 %copy-start.11 = (f32[192]{0:T(256)S(1)}, f32[192]{0:T(256)}, u32[]{:S(2)}) copy-start(f32[192]{0:T(256)} %param.24) | copy-start | bytes 2308
  230.6 36.1 %copy-start.8 = (bf16[192,32]{0,1:T(8,128)(2,1)S(1)}, bf16[192,32]{0,1:T(8,128)(2,1)}, u32[]{:S(2)}) copy-start(bf16[192,32]{0,1:T(8,128)(2,1)} %param.22) | copy-start | bytes 36868
  235.5 6.3 %collective-permute-start = (bf16[1,32,192]{2,1,0:T(8,128)(2,1)S(1)}, bf16[1,32,192]{2,1,0:T(8,128)(2,1)S(1)}, u32[]{:S(2)}, u32[]{:S(2)}) collective-permute-start(bf16[1,32,192]{2,1,0:T(8,128)(2,1)S(1)} %get-tuple-element.307), channel_id=1, source_target_pairs={{0,4},{4,8},{8,12},{1,5},{5,9},{9,13},{2,6},{6,10},{10,14},{3,7},{... | collective-permute-start | bytes 36872 | tf_op jit(solution)/shard_map/ppermute | solution.py:30
  239.2 5.6 %collective-permute-start.1 = (bf16[1,32,192]{2,1,0:T(8,128)(2,1)S(1)}, bf16[1,32,192]{2,1,0:T(8,128)(2,1)S(1)}, u32[]{:S(2)}, u32[]{:S(2)}) collective-permute-start(bf16[1,32,192]{2,1,0:T(8,128)(2,1)S(1)} %get-tuple-element.308), channel_id=1, source_target_pairs={{4,0},{8,4},{12,8},{5,1},{9,5},{13,9},{6,2},{10,6},{14,10},{7,3},{... | collective-permute-start | bytes 36872 | tf_op jit(solution)/shard_map/ppermute | solution.py:33
  244.8 4.8 %collective-permute-start.2 = (bf16[18,1,192]{2,1,0:T(2,128)(2,1)S(1)}, bf16[18,1,192]{2,1,0:T(2,128)(2,1)S(1)}, u32[]{:S(2)}, u32[]{:S(2)}) collective-permute-start(bf16[18,1,192]{2,1,0:T(2,128)(2,1)S(1)} %get-tuple-element.303), channel_id=1, source_target_pairs={{0,2},{1,3},{4,6},{5,7},{8,10},{9,11},{12,14},{13,15},{16,18},{17,... | collective-permute-start | bytes 20744 | tf_op jit(solution)/shard_map/ppermute | solution.py:30
  248.2 5.7 %collective-permute-start.3 = (bf16[18,1,192]{2,1,0:T(2,128)(2,1)S(1)}, bf16[18,1,192]{2,1,0:T(2,128)(2,1)S(1)}, u32[]{:S(2)}, u32[]{:S(2)}) collective-permute-start(bf16[18,1,192]{2,1,0:T(2,128)(2,1)S(1)} %get-tuple-element.304), channel_id=1, source_target_pairs={{2,0},{3,1},{6,4},{7,5},{10,8},{11,9},{14,12},{15,13},{18,16},{19,... | collective-permute-start | bytes 20744 | tf_op jit(solution)/shard_map/ppermute | solution.py:33
  255.4 10.5 %all-to-all-start = ((bf16[16,32,192]{2,0,1:T(8,128)(2,1)}), bf16[16,32,192]{2,0,1:T(8,128)(2,1)S(1)}, u32[]{:S(2)}, u32[]{:S(2)}) async-start(bf16[16,32,192]{2,0,1:T(8,128)(2,1)} %copy.47), calls=%async_computation | async-start | bytes 524288 | tf_op jit(solution)/shard_map/all_to_all | solution.py:124
  265.9 0.7 copy-start.1
  347.1 6.2 %copy-start.2 = (bf16[16,4,8,192]{3,2,0,1:T(8,128)(2,1)S(1)}, bf16[16,4,8,192]{3,2,0,1:T(8,128)(2,1)}, u32[]{:S(2)}) copy-start(bf16[16,4,8,192]{3,2,0,1:T(8,128)(2,1)} %copy-done.1) | copy-start | bytes 589828
  347.1 24.3 %copy-start.6 = (bf16[16,32,192]{2,1,0:T(8,128)(2,1)S(1)}, bf16[16,32,192]{2,1,0:T(8,128)(2,1)}, u32[]{:S(2)}) copy-start(bf16[16,32,192]{2,1,0:T(8,128)(2,1)} %param.17) | copy-start | bytes 589828
Sparse Core Ops, SparseCore 0:
  9.7 20.9 all-reduce.23
